TPU v7x, 128 devices: a whole 4x4x4 slice. The times are simulated.
128 devices in a mesh: blk: 8 (over z_lo, x), head: 16 (over y, z_hi, core).
Axes of the slice: x: 4, y: 4, z: 4 (z_hi: 2, z_lo: 2; z = z_hi * 2 + z_lo), core: 2. Of those that a mesh axis runs over, the one named last changes fastest.
Arguments:
- qkv: bfloat16 [32768, 6144], P(('blk', 'head')), may hold values from -12 to 12
Outputs:
- attended: bfloat16 [32768, 2048], P(('blk', 'head'))
All inputs are finite; a program needn't handle non-finite values.
Results may differ from a plain program's by a relative error of at most 0.0059.
Values may be sent and summed in bfloat16 or wider, within the bound.
A program may use at most 128 MiB of HBM per device.

v0:
```python
import jax
import jax.numpy as jnp
from jax import lax
from jax.sharding import PartitionSpec as P

HEAD_DIM = 64
BLOCK = 2048
BLK_DEV = 2


def attend(query, pair):
    keys = pair[:, 0]
    values = pair[:, 1]
    tile = min(512, BLOCK)
    scale = HEAD_DIM ** (-0.5)

    def one_tile(query_tile):
        scores = (
            jnp.einsum("qhd,khd->hqk", query_tile, keys, preferred_element_type=jnp.float32) * scale
        )
        row_max = jnp.max(scores, axis=-1)
        probs = jnp.exp(scores - row_max[..., None]).astype(jnp.bfloat16)
        total = jnp.sum(probs.astype(jnp.float32), axis=-1)
        weighted = jnp.einsum("hqk,khd->hqd", probs, values, preferred_element_type=jnp.float32)
        return (row_max, total, weighted)

    tiles = query.reshape(BLOCK // tile, tile, query.shape[1], query.shape[2])
    return lax.map(one_tile, tiles)


def combine(partials):
    overall = partials[0][0]
    for entry in partials[1:]:
        overall = jnp.maximum(overall, entry[0])
    numer = jnp.zeros_like(partials[0][2])
    denom = jnp.zeros_like(partials[0][1])
    for row_max, total, weighted in partials:
        factor = jnp.exp(row_max - overall)
        numer = numer + factor[..., None] * weighted
        denom = denom + factor * total
    result = numer / denom[..., None]
    return result.transpose(0, 2, 1, 3).reshape(BLOCK, result.shape[1] * result.shape[3])


def on_device(qkv):
    rows = qkv.shape[0]
    heads_cols = qkv.shape[1] // 3
    shaped = qkv.reshape(rows, 3, heads_cols)
    grouped = lax.all_to_all(shaped, "head", split_axis=2, concat_axis=0, tiled=True)
    local_cols = grouped.shape[2]
    heads_here = local_cols // HEAD_DIM
    grid = grouped.reshape(BLK_DEV, BLOCK, 3, heads_here, HEAD_DIM)
    queries = grid[:, :, 0]
    pairs = grid[:, :, 1:3]
    device_bits = lax.axis_size("blk").bit_length() - 1
    partials = [[] for j in range(BLK_DEV)]

    def own_blocks():
        for j in range(BLK_DEV):
            partials[j].append(attend(queries[j], pairs[j]))
            partials[j].append(attend(queries[j], pairs[j ^ 1 << 0]))

    gathered = lax.all_gather(pairs, "blk", axis=0, tiled=True)
    mine = lax.axis_index("blk")
    for bit in range(device_bits):
        for j in range(BLK_DEV):
            where = jnp.bitwise_xor(mine, 1 << bit) * BLK_DEV + j
            chosen = lax.dynamic_index_in_dim(gathered, where, 0, keepdims=False)
            partials[j].append(attend(queries[j], chosen))
    own_blocks()
    outputs = jnp.concatenate([combine(partials[j]) for j in range(BLK_DEV)], axis=0).astype(
        jnp.bfloat16
    )
    return lax.all_to_all(outputs, "head", split_axis=0, concat_axis=1, tiled=True)


def solution(mesh):
    in_specs = (P(("blk", "head"), None),)
    out_specs = P(("blk", "head"), None)
    return jax.shard_map(
        on_device, mesh=mesh, in_specs=in_specs, out_specs=out_specs, check_vma=False
    )
```

profile of v0, /device:TPU:1, one launch (start us, length us, event | category | flops | bytes accessed | tf_op | source)
XLA Modules:
  0.0 471.0 jit_solution(7720879860149030022)
XLA Ops:
  6.5 3.2 copy.39
  9.7 17.2 %copy.40 = bf16[256,3,2048]{0,1,2:T(4,128)(2,1)} copy(bf16[256,3,2048]{0,2,1:T(8,128)(2,1)S(1)} %bitcast.366) | data formatting | bytes 6291456 | tf_op jit(solution)/shard_map/reshape | solution.py:48
  26.9 9.3 %all-to-all-start = ((bf16[256,3,2048]{0,1,2:T(4,128)(2,1)}), bf16[256,3,2048]{0,1,2:T(4,128)(2,1)}, u32[]{:S(2)}, u32[]{:S(2)}) async-start(bf16[256,3,2048]{0,1,2:T(4,128)(2,1)} %copy.40), calls=%async_computation | async-start | bytes 8388608 | tf_op jit(solution)/shard_map/all_to_all | solution.py:49
  36.2 52.6 %all-to-all-done = bf16[256,3,2048]{0,1,2:T(4,128)(2,1)} async-done(((bf16[256,3,2048]{0,1,2:T(4,128)(2,1)}), bf16[256,3,2048]{0,1,2:T(4,128)(2,1)}, u32[]{:S(2)}, u32[]{:S(2)}) %all-to-all-start) | async-done | bytes 3145760 | tf_op jit(solution)/shard_map/all_to_all | solution.py:49
  91.5 3.5 copy.42
  95.0 3.9 reshape.47
  100.8 5.2 %slice_reduce_fusion.1 = (bf16[2048,2,64]{0,2,1:T(8,128)(2,1)}, bf16[2048,2,64]{0,2,1:T(8,128)(2,1)}) fusion(bf16[2,2048,3,2,64]{1,0,4,3,2:T(2,128)(2,1)S(1)} %reshape.47), kind=kLoop, calls=%fused_computation.121 | loop fusion | bytes 2097152 | tf_op jit(solution)/shard_map/slice | solution.py:69
  106.0 4.2 fusion.62
  114.7 2.9 copy_bitcast_fusion
  118.9 21.6 %while.143 = (s32[]{:T(128)}, f32[4,2,512]{2,1,0:T(2,128)S(1)}, f32[4,2,512]{2,1,0:T(2,128)S(1)}, f32[4,2,512,64]{2,3,1,0:T(8,128)}, bf16[4,512,2,64]{1,3,2,0:T(...) while((s32[]{:T(128)}, f32[4,2,512]{2,1,0:T(2,128)S(1)}, ...), condition=%wide.region_15.16_spmd, body=%wide.region_12.15_spmd.sunk | while | flops 557840384 | bytes 26640988 | solution.py:28
  141.7 21.9 %while.144 = (s32[]{:T(128)}, f32[4,2,512]{2,1,0:T(2,128)S(1)}, f32[4,2,512]{2,1,0:T(2,128)S(1)}, f32[4,2,512,64]{2,3,1,0:T(8,128)}, bf16[4,512,2,64]{1,3,2,0:T(...) while((s32[]{:T(128)}, f32[4,2,512]{2,1,0:T(2,128)S(1)}, ...), condition=%wide.region_19.20_spmd, body=%wide.region_16.19_spmd.sunk | while | flops 557840384 | bytes 26640988 | solution.py:28
  164.7 21.6 %while.148 = (s32[]{:T(128)}, f32[4,2,512]{2,1,0:T(2,128)S(1)}, f32[4,2,512]{2,1,0:T(2,128)S(1)}, f32[4,2,512,64]{2,3,1,0:T(8,128)}, bf16[4,512,2,64]{1,3,2,0:T(...) while((s32[]{:T(128)}, f32[4,2,512]{2,1,0:T(2,128)S(1)}, ...), condition=%wide.region_35.36_spmd, body=%wide.region_32.35_spmd.sunk | while | flops 557840384 | bytes 26640988 | solution.py:28
  186.9 19.9 %while.149 = (s32[]{:T(128)}, f32[4,2,512]{2,1,0:T(2,128)S(1)}, f32[4,2,512]{2,1,0:T(2,128)S(1)}, f32[4,2,512,64]{2,3,1,0:T(8,128)S(1)}, bf16[4,512,2,64]{1,3,2,...) while((s32[]{:T(128)}, f32[4,2,512]{2,1,0:T(2,128)S(1)}, ...), condition=%wide.region_39.40_spmd, body=%wide.region_36.39_spmd.sunk | while | flops 557840384 | bytes 26640480 | solution.py:28
  206.8 83.2 %all-gather.2.cloned.1.call-done = bf16[16,2048,2,2,64]{1,4,3,2,0:T(8,128)(2,1)} async-done(((bf16[2,2048,2,2,64]{1,4,3,2,0:T(8,128)(2,1)}), bf16[16,2048,2,2,64]{1,4,3,2,0:T(8,128)(2,1)}) %all-gather.2.cloned.1.call-update) | async-done | bytes 16777232 | tf_op jit(solution)/shard_map/all_gather | solution.py:63
  290.1 5.3 %dynamic-slice_bitcast_fusion.5 = (bf16[2048,2,2,64]{0,3,2,1:T(8,128)(2,1)S(1)}, bf16[2048,2,2,64]{0,3,2,1:T(8,128)(2,1)}, bf16[2048,2,2,64]{0,3,2,1:T(8,128)(2,...) fusion(bf16[16,2048,2,2,64]{1,4,3,2,0:T(8,128)(2,1)} %all-gather.2., ...), kind=kLoop, calls=%fused_computation.132 | loop fusion | bytes 12582936 | tf_op jit(solution)/shard_map/jit(dynamic_index_in_dim)/squeeze | solution.py:68
  296.9 22.0 %while.140 = (s32[]{:T(128)}, f32[4,2,512]{2,1,0:T(2,128)S(1)}, f32[4,2,512]{2,1,0:T(2,128)S(1)}, f32[4,2,512,64]{2,3,1,0:T(8,128)}, bf16[4,512,2,64]{1,3,2,0:T(...) while((s32[]{:T(128)}, f32[4,2,512]{2,1,0:T(2,128)S(1)}, ...), condition=%wide.region_3.4_spmd, body=%wide.region_0.3_spmd.sunk | while | flops 557840384 | bytes 26640988 | solution.py:28
  319.1 19.9 %while.141 = (s32[]{:T(128)}, f32[4,2,512]{2,1,0:T(2,128)S(1)}, f32[4,2,512]{2,1,0:T(2,128)S(1)}, f32[4,2,512,64]{2,3,1,0:T(8,128)S(1)}, bf16[4,512,2,64]{1,3,2,...) while((s32[]{:T(128)}, f32[4,2,512]{2,1,0:T(2,128)S(1)}, ...), condition=%wide.region_7.8_spmd, body=%wide.region_4.7_spmd.sunk | while | flops 557840384 | bytes 26640480 | solution.py:28
  342.8 21.6 %while.142 = (s32[]{:T(128)}, f32[4,2,512]{2,1,0:T(2,128)S(1)}, f32[4,2,512]{2,1,0:T(2,128)S(1)}, f32[4,2,512,64]{2,3,1,0:T(8,128)}, bf16[4,512,2,64]{1,3,2,0:T(...) while((s32[]{:T(128)}, f32[4,2,512]{2,1,0:T(2,128)S(1)}, ...), condition=%wide.region_11.12_spmd, body=%wide.region_8.11_spmd.sunk | while | flops 557840384 | bytes 26640988 | solution.py:28
  364.4 3.2 fusion.60
  368.3 20.1 %while.145 = (s32[]{:T(128)}, f32[4,2,512]{2,1,0:T(2,128)S(1)}, f32[4,2,512]{2,1,0:T(2,128)S(1)}, f32[4,2,512,64]{2,3,1,0:T(8,128)S(1)}, bf16[4,512,2,64]{1,3,2,...) while((s32[]{:T(128)}, f32[4,2,512]{2,1,0:T(2,128)S(1)}, ...), condition=%wide.region_23.24_spmd, body=%wide.region_20.23_spmd.sunk | while | flops 557840384 | bytes 26640480 | solution.py:28
  392.2 21.6 %while.146 = (s32[]{:T(128)}, f32[4,2,512]{2,1,0:T(2,128)S(1)}, f32[4,2,512]{2,1,0:T(2,128)S(1)}, f32[4,2,512,64]{2,3,1,0:T(8,128)}, bf16[4,512,2,64]{1,3,2,0:T(...) while((s32[]{:T(128)}, f32[4,2,512]{2,1,0:T(2,128)S(1)}, ...), condition=%wide.region_27.28_spmd, body=%wide.region_24.27_spmd.sunk | while | flops 557840384 | bytes 26640988 | solution.py:28
  414.0 19.9 %while.147 = (s32[]{:T(128)}, f32[4,2,512]{2,1,0:T(2,128)S(1)}, f32[4,2,512]{2,1,0:T(2,128)S(1)}, f32[4,2,512,64]{2,3,1,0:T(8,128)S(1)}, bf16[4,512,2,64]{1,3,2,...) while((s32[]{:T(128)}, f32[4,2,512]{2,1,0:T(2,128)S(1)}, ...), condition=%wide.region_31.32_spmd, body=%wide.region_28.31_spmd.sunk | while | flops 557840384 | bytes 26640480 | solution.py:28
  434.0 2.9 fusion.61
  438.2 23.8 %all_to_all.31 = bf16[16,256,128]{2,1,0:T(8,128)(2,1)S(1)} all-to-all(bf16[16,256,128]{2,1,0:T(8,128)(2,1)S(1)} %bitcast.367), channel_id=1, replica_groups=mesh['blk'=8,'head'=16] {'head'}, dimensions={0} | all-to-all | bytes 2097152 | tf_op jit(solution)/shard_map/all_to_all | solution.py:74
  (252 shorter events, 234.8 us)
Async XLA Ops:
  26.9 62.0 %all-to-all-start = ((bf16[256,3,2048]{0,1,2:T(4,128)(2,1)}), bf16[256,3,2048]{0,1,2:T(4,128)(2,1)}, u32[]{:S(2)}, u32[]{:S(2)}) async-start(bf16[256,3,2048]{0,1,2:T(4,128)(2,1)} %copy.40), calls=%async_computation | async-start | bytes 8388608 | tf_op jit(solution)/shard_map/all_to_all | solution.py:49
  36.2 253.9 %all-gather.2.cloned.1.call-start = ((), (), s32[]{:S(2)}) async-start(), calls=%async_computation.2 | async-start | bytes 18874368 | tf_op jit(solution)/shard_map/all_gather | solution.py:63
  110.2 4.5 copy-start
  140.5 1.2 copy-start.4
  140.5 1.2 copy-start.6
  163.6 1.1 copy-start.8
  163.6 1.1 copy-start.10
  186.3 0.6 copy-start.12
  186.3 0.6 copy-start.14
  206.8 88.6 %copy-start.1 = (f32[4,2,512,64]{2,3,1,0:T(8,128)}, f32[4,2,512,64]{2,3,1,0:T(8,128)S(1)}, u32[]{:S(2)}) copy-start(f32[4,2,512,64]{2,3,1,0:T(8,128)S(1)} %get-tuple-element.419) | copy-start | bytes 3145732
  206.8 88.9 %copy-start.16 = (f32[4,2,512]{2,1,0:T(2,128)}, f32[4,2,512]{2,1,0:T(2,128)S(1)}, u32[]{:S(2)}) copy-start(f32[4,2,512]{2,1,0:T(2,128)S(1)} %get-tuple-element.414) | copy-start | bytes 49156
  206.8 88.9 %copy-start.18 = (f32[4,2,512]{2,1,0:T(2,128)}, f32[4,2,512]{2,1,0:T(2,128)S(1)}, u32[]{:S(2)}) copy-start(f32[4,2,512]{2,1,0:T(2,128)S(1)} %get-tuple-element.424) | copy-start | bytes 49156
  339.0 1.0 copy-start.2
  342.7 21.6 %copy-start.5 = (f32[4,2,512]{2,1,0:T(2,128)S(1)}, f32[4,2,512]{2,1,0:T(2,128)}, u32[]{:S(2)}) copy-start(f32[4,2,512]{2,1,0:T(2,128)} %copy-done.4) | copy-start | bytes 49156
  342.7 21.6 %copy-start.7 = (f32[4,2,512]{2,1,0:T(2,128)S(1)}, f32[4,2,512]{2,1,0:T(2,128)}, u32[]{:S(2)}) copy-start(f32[4,2,512]{2,1,0:T(2,128)} %copy-done.6) | copy-start | bytes 49156
  342.8 21.6 %copy-start.9 = (f32[4,2,512]{2,1,0:T(2,128)S(1)}, f32[4,2,512]{2,1,0:T(2,128)}, u32[]{:S(2)}) copy-start(f32[4,2,512]{2,1,0:T(2,128)} %copy-done.8) | copy-start | bytes 49156
  342.8 21.6 %copy-start.11 = (f32[4,2,512]{2,1,0:T(2,128)S(1)}, f32[4,2,512]{2,1,0:T(2,128)}, u32[]{:S(2)}) copy-start(f32[4,2,512]{2,1,0:T(2,128)} %copy-done.10) | copy-start | bytes 49156
  388.4 1.0 copy-start.3
  414.0 20.0 %copy-start.13 = (f32[4,2,512]{2,1,0:T(2,128)S(1)}, f32[4,2,512]{2,1,0:T(2,128)}, u32[]{:S(2)}) copy-start(f32[4,2,512]{2,1,0:T(2,128)} %copy-done.12) | copy-start | bytes 49156
  414.0 20.0 %copy-start.15 = (f32[4,2,512]{2,1,0:T(2,128)S(1)}, f32[4,2,512]{2,1,0:T(2,128)}, u32[]{:S(2)}) copy-start(f32[4,2,512]{2,1,0:T(2,128)} %copy-done.14) | copy-start | bytes 49156
  414.0 20.0 %copy-start.17 = (f32[4,2,512]{2,1,0:T(2,128)S(1)}, f32[4,2,512]{2,1,0:T(2,128)}, u32[]{:S(2)}) copy-start(f32[4,2,512]{2,1,0:T(2,128)} %copy-done.16) | copy-start | bytes 49156
  414.0 20.0 %copy-start.19 = (f32[4,2,512]{2,1,0:T(2,128)S(1)}, f32[4,2,512]{2,1,0:T(2,128)}, u32[]{:S(2)}) copy-start(f32[4,2,512]{2,1,0:T(2,128)} %copy-done.18) | copy-start | bytes 49156
Sparse Core Ops, SparseCore 0:
  112.6 177.4 all-gather.1
where the time goes:
time: 477 us; the launch traced here: 471 us
  matrix products  142 us (30%)
  waiting for transfers between devices  136 us (29%)
  local copies, waits for them, and re-layouts  72 us (15%)
  other arithmetic  71.9 us (15%)
  blocking collectives  23.8 us (5%)
  between operations  14.1 us (3%)
  starting transfers between devices  9.34 us (2%)
    dot_general x40, matrix products, one_tile(): jnp.einsum('hqk,khd->hqd', probs, values, preferred_element_type=jnp.floa...  87 us
    all_gather x1, waiting for transfers between devices, on_device(): gathered = lax.all_gather(pairs, 'blk', axis=0, tiled=True)  83.2 us
    reduce_sum x40, other arithmetic, one_tile(): total = jnp.sum(probs.astype(jnp.float32), axis=-1)  65.6 us
    dot_general x40, matrix products, one_tile(): jnp.einsum('qhd,khd->hqk', query_tile, keys, preferred_element_type=jnp.f...  55.4 us
    all_to_all x1, waiting for transfers between devices, on_device(): lax.all_to_all(shaped, 'head', split_axis=2, concat_axis=0, tiled=True)  52.6 us
    all_to_all x1, blocking collectives, on_device(): lax.all_to_all(outputs, 'head', split_axis=0, concat_axis=1, tiled=True)  23.8 us
    reshape x1, local copies, waits for them, and re-layouts, on_device(): shaped = qkv.reshape(rows, 3, heads_cols)  17.2 us
  transfers between devices with their start and end apart: 2, of which 2 were waited for; matrix products, arithmetic and copies ran while one was open for 20% of the time, Pallas kernels for 0%

commit v1 on v0

--- a/solution.py
+++ b/solution.py
@@ -46,7 +46,10 @@
     rows = qkv.shape[0]
     heads_cols = qkv.shape[1] // 3
     shaped = qkv.reshape(rows, 3, heads_cols)
-    grouped = lax.all_to_all(shaped, "head", split_axis=2, concat_axis=0, tiled=True)
+    grouped = jnp.concatenate(
+        lax.all_to_all(jnp.stack(jnp.split(shaped, lax.axis_size("head"), axis=2)), "head", 0, 0),
+        axis=0,
+    )
     local_cols = grouped.shape[2]
     heads_here = local_cols // HEAD_DIM
     grid = grouped.reshape(BLK_DEV, BLOCK, 3, heads_here, HEAD_DIM)

time: 477 us -> 450 us (0.943)
  waiting for transfers between devices: 136 us -> 119 us
  local copies, waits for them, and re-layouts: 72 us -> 63.9 us
    reshape x2 -> x0, local copies, waits for them, and re-layouts: 21.1 us -> none  [the longest x1 17.2 us: on_device(): shaped = qkv.reshape(rows, 3, heads_cols)]
    all_to_all x1, waiting for transfers between devices: 52.6 us -> 39.7 us  [on_device(): lax.all_to_all(jnp.stack(jnp.split(shaped, lax.axis_size('head'), axis=2)...]
    unnamed x44 -> x61, local copies, waits for them, and re-layouts: 8.72 us -> 19.8 us
    another operation x30 -> x32, local copies, waits for them, and re-layouts: 7.37 us -> 12 us
  transfers between devices with their start and end apart: 2 -> 2, of which waited for: 2 -> 2; matrix products, arithmetic and copies ran while one was open for 20% -> 21% of each run, Pallas kernels for 0% -> 0%
where the time goes in v1:
time: 450 us; the launch traced here: 447 us
  matrix products  142 us (32%)
  waiting for transfers between devices  119 us (26%)
  other arithmetic  72 us (16%)
  local copies, waits for them, and re-layouts  63.9 us (14%)
  blocking collectives  23.8 us (5%)
  between operations  14.1 us (3%)
  starting transfers between devices  9.34 us (2%)
    dot_general x40, matrix products, one_tile(): jnp.einsum('hqk,khd->hqd', probs, values, preferred_element_type=jnp.floa...  87 us
    all_gather x1, waiting for transfers between devices, on_device(): gathered = lax.all_gather(pairs, 'blk', axis=0, tiled=True)  79.8 us
    reduce_sum x40, other arithmetic, one_tile(): total = jnp.sum(probs.astype(jnp.float32), axis=-1)  65.6 us
    dot_general x40, matrix products, one_tile(): jnp.einsum('qhd,khd->hqk', query_tile, keys, preferred_element_type=jnp.f...  55.4 us
    all_to_all x1, waiting for transfers between devices, on_device(): lax.all_to_all(jnp.stack(jnp.split(shaped, lax.axis_size('head'), axis=2)...  39.7 us
    all_to_all x1, blocking collectives, on_device(): lax.all_to_all(outputs, 'head', split_axis=0, concat_axis=1, tiled=True)  23.8 us
    unnamed x61, local copies, waits for them, and re-layouts  19.8 us
    all_to_all x1, starting transfers between devices, on_device(): lax.all_to_all(jnp.stack(jnp.split(shaped, lax.axis_size('head'), axis=2)...  9.3 us
  transfers between devices with their start and end apart: 2, of which 2 were waited for; matrix products, arithmetic and copies ran while one was open for 21% of the time, Pallas kernels for 0%

profile of v1, /device:TPU:1, one launch (start us, length us, event | category | flops | bytes accessed | tf_op | source)
XLA Modules:
  0.0 446.6 jit_solution(14690774674157875450)
XLA Ops:
  6.5 3.2 copy.39
  20.7 9.3 %all-to-all-start = ((bf16[16,256,3,128]{1,3,2,0:T(8,128)(2,1)}), bf16[16,256,3,128]{1,3,2,0:T(8,128)(2,1)S(1)}, u32[]{:S(2)}, u32[]{:S(2)}) async-start(bf16[16,256,3,128]{1,3,2,0:T(8,128)(2,1)} %fusion.62), calls=%async_computation | async-start | bytes 6291456 | tf_op jit(solution)/shard_map/all_to_all | solution.py:50
  30.1 39.7 %all-to-all-done = bf16[16,256,3,128]{1,3,2,0:T(8,128)(2,1)S(1)} async-done(((bf16[16,256,3,128]{1,3,2,0:T(8,128)(2,1)}), bf16[16,256,3,128]{1,3,2,0:T(8,128)(2,1)S(1)}, u32[]{:S(2)}, u32[]{:S(2)}) %all-to-all-start) | async-done | bytes 3145760 | tf_op jit(solution)/shard_map/all_to_all | solution.py:50
  69.8 3.4 copy.40
  73.2 3.9 reshape_reshape.3
  79.0 5.2 %slice_reduce_fusion.1 = (bf16[2048,2,64]{0,2,1:T(8,128)(2,1)}, bf16[2048,2,64]{0,2,1:T(8,128)(2,1)}) fusion(bf16[2,2048,3,2,64]{1,0,4,3,2:T(2,128)(2,1)S(1)} %reshape_reshape.3), kind=kLoop, calls=%fused_computation.121 | loop fusion | bytes 2097152 | tf_op jit(solution)/shard_map/slice | solution.py:72
  84.2 4.2 fusion.78
  92.9 2.9 copy_bitcast_fusion
  97.1 21.7 %while.143 = (s32[]{:T(128)}, f32[4,2,512]{2,1,0:T(2,128)S(1)}, f32[4,2,512]{2,1,0:T(2,128)S(1)}, f32[4,2,512,64]{2,3,1,0:T(8,128)}, bf16[4,512,2,64]{1,3,2,0:T(...) while((s32[]{:T(128)}, f32[4,2,512]{2,1,0:T(2,128)S(1)}, ...), condition=%wide.region_15.16_spmd, body=%wide.region_12.15_spmd.sunk | while | flops 557840384 | bytes 26640988 | solution.py:28
  119.9 21.9 %while.144 = (s32[]{:T(128)}, f32[4,2,512]{2,1,0:T(2,128)S(1)}, f32[4,2,512]{2,1,0:T(2,128)S(1)}, f32[4,2,512,64]{2,3,1,0:T(8,128)}, bf16[4,512,2,64]{1,3,2,0:T(...) while((s32[]{:T(128)}, f32[4,2,512]{2,1,0:T(2,128)S(1)}, ...), condition=%wide.region_19.20_spmd, body=%wide.region_16.19_spmd.sunk | while | flops 557840384 | bytes 26640988 | solution.py:28
  128.6 2.4 fusion.143
  142.9 21.6 %while.148 = (s32[]{:T(128)}, f32[4,2,512]{2,1,0:T(2,128)S(1)}, f32[4,2,512]{2,1,0:T(2,128)S(1)}, f32[4,2,512,64]{2,3,1,0:T(8,128)}, bf16[4,512,2,64]{1,3,2,0:T(...) while((s32[]{:T(128)}, f32[4,2,512]{2,1,0:T(2,128)S(1)}, ...), condition=%wide.region_35.36_spmd, body=%wide.region_32.35_spmd.sunk | while | flops 557840384 | bytes 26640988 | solution.py:28
  165.1 19.9 %while.149 = (s32[]{:T(128)}, f32[4,2,512]{2,1,0:T(2,128)S(1)}, f32[4,2,512]{2,1,0:T(2,128)S(1)}, f32[4,2,512,64]{2,3,1,0:T(8,128)S(1)}, bf16[4,512,2,64]{1,3,2,...) while((s32[]{:T(128)}, f32[4,2,512]{2,1,0:T(2,128)S(1)}, ...), condition=%wide.region_39.40_spmd, body=%wide.region_36.39_spmd.sunk | while | flops 557840384 | bytes 26640480 | solution.py:28
  185.0 79.8 %all-gather.2.cloned.1.call-done = bf16[16,2048,2,2,64]{1,4,3,2,0:T(8,128)(2,1)} async-done(((bf16[2,2048,2,2,64]{1,4,3,2,0:T(8,128)(2,1)}), bf16[16,2048,2,2,64]{1,4,3,2,0:T(8,128)(2,1)}) %all-gather.2.cloned.1.call-update) | async-done | bytes 16777232 | tf_op jit(solution)/shard_map/all_gather | solution.py:66
  264.8 5.3 %dynamic-slice_bitcast_fusion.5 = (bf16[2048,2,2,64]{0,3,2,1:T(8,128)(2,1)S(1)}, bf16[2048,2,2,64]{0,3,2,1:T(8,128)(2,1)}, bf16[2048,2,2,64]{0,3,2,1:T(8,128)(2,...) fusion(bf16[16,2048,2,2,64]{1,4,3,2,0:T(8,128)(2,1)} %all-gather.2., ...), kind=kLoop, calls=%fused_computation.132 | loop fusion | bytes 12582936 | tf_op jit(solution)/shard_map/jit(dynamic_index_in_dim)/squeeze | solution.py:71
  271.5 22.0 %while.140 = (s32[]{:T(128)}, f32[4,2,512]{2,1,0:T(2,128)S(1)}, f32[4,2,512]{2,1,0:T(2,128)S(1)}, f32[4,2,512,64]{2,3,1,0:T(8,128)}, bf16[4,512,2,64]{1,3,2,0:T(...) while((s32[]{:T(128)}, f32[4,2,512]{2,1,0:T(2,128)S(1)}, ...), condition=%wide.region_3.4_spmd, body=%wide.region_0.3_spmd.sunk | while | flops 557840384 | bytes 26640988 | solution.py:28
  293.7 19.9 %while.141 = (s32[]{:T(128)}, f32[4,2,512]{2,1,0:T(2,128)S(1)}, f32[4,2,512]{2,1,0:T(2,128)S(1)}, f32[4,2,512,64]{2,3,1,0:T(8,128)S(1)}, bf16[4,512,2,64]{1,3,2,...) while((s32[]{:T(128)}, f32[4,2,512]{2,1,0:T(2,128)S(1)}, ...), condition=%wide.region_7.8_spmd, body=%wide.region_4.7_spmd.sunk | while | flops 557840384 | bytes 26640480 | solution.py:28
  317.4 21.6 %while.142 = (s32[]{:T(128)}, f32[4,2,512]{2,1,0:T(2,128)S(1)}, f32[4,2,512]{2,1,0:T(2,128)S(1)}, f32[4,2,512,64]{2,3,1,0:T(8,128)}, bf16[4,512,2,64]{1,3,2,0:T(...) while((s32[]{:T(128)}, f32[4,2,512]{2,1,0:T(2,128)S(1)}, ...), condition=%wide.region_11.12_spmd, body=%wide.region_8.11_spmd.sunk | while | flops 557840384 | bytes 26640988 | solution.py:28
  339.0 3.3 fusion.60
  343.8 20.1 %while.145 = (s32[]{:T(128)}, f32[4,2,512]{2,1,0:T(2,128)S(1)}, f32[4,2,512]{2,1,0:T(2,128)S(1)}, f32[4,2,512,64]{2,3,1,0:T(8,128)S(1)}, bf16[4,512,2,64]{1,3,2,...) while((s32[]{:T(128)}, f32[4,2,512]{2,1,0:T(2,128)S(1)}, ...), condition=%wide.region_23.24_spmd, body=%wide.region_20.23_spmd.sunk | while | flops 557840384 | bytes 26640480 | solution.py:28
  367.6 21.6 %while.146 = (s32[]{:T(128)}, f32[4,2,512]{2,1,0:T(2,128)S(1)}, f32[4,2,512]{2,1,0:T(2,128)S(1)}, f32[4,2,512,64]{2,3,1,0:T(8,128)}, bf16[4,512,2,64]{1,3,2,0:T(...) while((s32[]{:T(128)}, f32[4,2,512]{2,1,0:T(2,128)S(1)}, ...), condition=%wide.region_27.28_spmd, body=%wide.region_24.27_spmd.sunk | while | flops 557840384 | bytes 26640988 | solution.py:28
  389.5 19.9 %while.147 = (s32[]{:T(128)}, f32[4,2,512]{2,1,0:T(2,128)S(1)}, f32[4,2,512]{2,1,0:T(2,128)S(1)}, f32[4,2,512,64]{2,3,1,0:T(8,128)S(1)}, bf16[4,512,2,64]{1,3,2,...) while((s32[]{:T(128)}, f32[4,2,512]{2,1,0:T(2,128)S(1)}, ...), condition=%wide.region_31.32_spmd, body=%wide.region_28.31_spmd.sunk | while | flops 557840384 | bytes 26640480 | solution.py:28
  409.5 3.0 fusion.61
  413.7 23.8 %all_to_all.21 = bf16[16,256,128]{2,1,0:T(8,128)(2,1)S(1)} all-to-all(bf16[16,256,128]{2,1,0:T(8,128)(2,1)S(1)} %bitcast.442), channel_id=1, replica_groups=mesh['blk'=8,'head'=16] {'head'}, dimensions={0} | all-to-all | bytes 2097152 | tf_op jit(solution)/shard_map/all_to_all | solution.py:77
  (268 shorter events, 241.6 us)
Async XLA Ops:
  20.7 49.1 %all-to-all-start = ((bf16[16,256,3,128]{1,3,2,0:T(8,128)(2,1)}), bf16[16,256,3,128]{1,3,2,0:T(8,128)(2,1)S(1)}, u32[]{:S(2)}, u32[]{:S(2)}) async-start(bf16[16,256,3,128]{1,3,2,0:T(8,128)(2,1)} %fusion.62), calls=%async_computation | async-start | bytes 6291456 | tf_op jit(solution)/shard_map/all_to_all | solution.py:50
  30.0 234.7 %all-gather.2.cloned.1.call-start = ((), (), s32[]{:S(2)}) async-start(), calls=%async_computation.2 | async-start | bytes 18874368 | tf_op jit(solution)/shard_map/all_gather | solution.py:66
  88.4 4.4 copy-start
  118.7 1.2 copy-start.5
  118.7 1.2 copy-start.7
  141.7 1.1 copy-start.9
  141.7 1.1 copy-start.11
  164.5 0.6 copy-start.13
  164.5 0.6 copy-start.15
  185.0 85.1 %copy-start.1 = (f32[4,2,512,64]{2,3,1,0:T(8,128)}, f32[4,2,512,64]{2,3,1,0:T(8,128)S(1)}, u32[]{:S(2)}) copy-start(f32[4,2,512,64]{2,3,1,0:T(8,128)S(1)} %get-tuple-element.419) | copy-start | bytes 3145732
  185.0 85.3 %copy-start.17 = (f32[4,2,512]{2,1,0:T(2,128)}, f32[4,2,512]{2,1,0:T(2,128)S(1)}, u32[]{:S(2)}) copy-start(f32[4,2,512]{2,1,0:T(2,128)S(1)} %get-tuple-element.414) | copy-start | bytes 49156
  185.0 85.3 %copy-start.19 = (f32[4,2,512]{2,1,0:T(2,128)}, f32[4,2,512]{2,1,0:T(2,128)S(1)}, u32[]{:S(2)}) copy-start(f32[4,2,512]{2,1,0:T(2,128)S(1)} %get-tuple-element.424) | copy-start | bytes 49156
  313.6 1.0 copy-start.2
  317.4 21.6 %copy-start.6 = (f32[4,2,512]{2,1,0:T(2,128)S(1)}, f32[4,2,512]{2,1,0:T(2,128)}, u32[]{:S(2)}) copy-start(f32[4,2,512]{2,1,0:T(2,128)} %copy-done.5) | copy-start | bytes 49156
  317.4 21.6 %copy-start.8 = (f32[4,2,512]{2,1,0:T(2,128)S(1)}, f32[4,2,512]{2,1,0:T(2,128)}, u32[]{:S(2)}) copy-start(f32[4,2,512]{2,1,0:T(2,128)} %copy-done.7) | copy-start | bytes 49156
  317.4 21.6 %copy-start.10 = (f32[4,2,512]{2,1,0:T(2,128)S(1)}, f32[4,2,512]{2,1,0:T(2,128)}, u32[]{:S(2)}) copy-start(f32[4,2,512]{2,1,0:T(2,128)} %copy-done.9) | copy-start | bytes 49156
  317.4 21.6 %copy-start.12 = (f32[4,2,512]{2,1,0:T(2,128)S(1)}, f32[4,2,512]{2,1,0:T(2,128)}, u32[]{:S(2)}) copy-start(f32[4,2,512]{2,1,0:T(2,128)} %copy-done.11) | copy-start | bytes 49156
  363.8 1.0 copy-start.3
  389.4 20.0 %copy-start.14 = (f32[4,2,512]{2,1,0:T(2,128)S(1)}, f32[4,2,512]{2,1,0:T(2,128)}, u32[]{:S(2)}) copy-start(f32[4,2,512]{2,1,0:T(2,128)} %copy-done.13) | copy-start | bytes 49156
  389.4 20.0 %copy-start.16 = (f32[4,2,512]{2,1,0:T(2,128)S(1)}, f32[4,2,512]{2,1,0:T(2,128)}, u32[]{:S(2)}) copy-start(f32[4,2,512]{2,1,0:T(2,128)} %copy-done.15) | copy-start | bytes 49156
  389.4 20.0 %copy-start.18 = (f32[4,2,512]{2,1,0:T(2,128)S(1)}, f32[4,2,512]{2,1,0:T(2,128)}, u32[]{:S(2)}) copy-start(f32[4,2,512]{2,1,0:T(2,128)} %copy-done.17) | copy-start | bytes 49156
  389.4 20.0 %copy-start.20 = (f32[4,2,512]{2,1,0:T(2,128)S(1)}, f32[4,2,512]{2,1,0:T(2,128)}, u32[]{:S(2)}) copy-start(f32[4,2,512]{2,1,0:T(2,128)} %copy-done.19) | copy-start | bytes 49156
  409.4 3.6 copy-start.4
Sparse Core Ops, SparseCore 0:
  90.8 173.9 all-gather.1
